TPU v7x, 256 devices: a whole 4x4x8 slice. The times are simulated.
256 devices in a mesh: blk: 64 (over y_lo, z, x), rep: 4 (over y_hi, core).
Axes of the slice: x: 4, y: 4 (y_hi: 2, y_lo: 2; y = y_hi * 2 + y_lo), z: 8, core: 2. Of those that a mesh axis runs over, the one named last changes fastest.
Arguments:
- features: bfloat16 [262144, 128], P(('blk', 'rep')), may hold values from -6 to 6
- weight: bfloat16 [128, 512], replicated, may hold values from -0.5 to 0.5
- bias: float32 [512], replicated, may hold values from -3 to 3
- tile_values: bfloat16 [262144, 4096], P(('blk', 'rep')), may hold values from -0.125 to 0.125
- tile_cols: int32 [2048, 32], P(('blk', 'rep')), may hold values from 0 to 95, as said below
- tile_counts: int32 [2048], P(('blk', 'rep')), may hold values from 1 to 32, as said below
- out_grad: bfloat16 [262144, 512], P(('blk', 'rep')), may hold values from -6 to 6
Outputs:
- activations: bfloat16 [262144, 512], P(('blk', 'rep'))
- feature_grad: float32 [262144, 128], P(('blk', 'rep'))
- weight_grad: float32 [128, 512], replicated
- bias_grad: float32 [512], replicated
Inputs may be any that keep to these rules, and one draw needn't show every extreme that they name: `tile_cols`: within one row tile the 32 entries are different. `tile_counts`: slots 0 to count - 1 of a row tile are live.
All inputs are finite; a program needn't handle non-finite values.
Results may differ from a plain program's by a relative error of at most 0.0059.
Values may be sent and summed in bfloat16 or wider, within the bound.
No kernel may reach another device: no remote copies, remote signals or barrier semaphores. Data moves between devices by JAX's collectives and lax.ppermute only.
A program may use at most 128 MiB of HBM per device.

v0:
```python
import math
import jax
import jax.numpy as jnp
from jax import lax
from jax.sharding import PartitionSpec as P

TILE = 128
REACH = 1
SLOTS = 32


def passed_along(value, axis, steps):
    count = lax.axis_size(axis)
    pairs = [(source, (source + steps) % count) for source in range(count)]
    return lax.ppermute(value, axis, pairs)


def in_blocks(shard, dim, length):
    before, after = (shard.shape[:dim], shard.shape[dim + 1 :])
    return jnp.moveaxis(shard.reshape(*before, length, -1, *after), dim, 0)


def summed_on_arrival(shard, axis, dim):
    length = lax.axis_size(axis)
    pieces = lax.all_to_all(in_blocks(shard, dim, length), axis, 0, 0, tiled=True)
    return jnp.sum(pieces, axis=0)


def gelu_parts(pre_act):
    inner = 0.7978845608028654 * (pre_act + 0.044715 * pre_act * pre_act * pre_act)
    tangent = jnp.tanh(inner)
    value_part = 0.5 * pre_act * (1.0 + tangent)
    slope = 0.5 * (1.0 + tangent) + 0.5 * pre_act * (
        1.0 - tangent * tangent
    ) * 0.7978845608028654 * (1.0 + 0.134145 * pre_act * pre_act)
    return (value_part, slope)


def on_device(features, weight, bias, tile_values, tile_cols, tile_counts, out_grad):
    rows_dev, in_dim = features.shape
    row_tiles = rows_dev // TILE
    group_size = lax.axis_size("rep")
    block_rows = rows_dev * group_size
    nodes = block_rows * lax.axis_size("blk")
    offsets = list(range(-REACH, REACH + 1))
    pieces = []
    for offset_now in offsets:
        if offset_now == 0:
            pieces.append(features)
        else:
            pieces.append(passed_along(features, "blk", -offset_now))
    stacked = jnp.stack(pieces)
    window = lax.all_gather(stacked, "rep", axis=1, tiled=True).reshape(-1, in_dim)
    window_tiles = window.reshape(-1, TILE, in_dim)
    is_live = jnp.arange(SLOTS)[None, :] < tile_counts[:, None]
    gathered = window_tiles[tile_cols]
    gathered = jnp.where(is_live[:, :, None, None], gathered, jnp.zeros((), gathered.dtype))
    gathered = gathered.reshape(row_tiles, SLOTS * TILE, in_dim)
    values = tile_values.reshape(row_tiles, TILE, SLOTS * TILE)
    summed = jnp.einsum(
        "rik,rkf->rif", values, gathered, preferred_element_type=jnp.float32
    ).reshape(rows_dev, in_dim)
    aggregated = summed.astype(jnp.bfloat16)
    pre_act = jnp.dot(aggregated, weight, preferred_element_type=jnp.float32) + bias
    value_part, slope = gelu_parts(pre_act)
    activations = value_part.astype(jnp.bfloat16)
    pre_grad = (out_grad.astype(jnp.float32) * slope).astype(jnp.bfloat16)
    factor = 1.0 / math.sqrt(nodes)
    local_weight = (
        lax.dot_general(
            aggregated, pre_grad, (((0,), (0,)), ((), ())), preferred_element_type=jnp.float32
        )
        * factor
    )
    local_bias = jnp.sum(pre_grad.astype(jnp.float32), axis=0) * factor
    weight_grad, bias_grad = lax.psum((local_weight, local_bias), ("blk", "rep"))
    row_grad = lax.dot_general(
        pre_grad, weight, (((1,), (1,)), ((), ())), preferred_element_type=jnp.float32
    ).astype(jnp.bfloat16)
    grad_tiles = row_grad.reshape(row_tiles, TILE, in_dim)
    partial_value = jnp.einsum(
        "rik,rif->rkf", values, grad_tiles, preferred_element_type=jnp.float32
    )
    partial_value = partial_value.reshape(row_tiles, SLOTS, TILE, in_dim)
    partial_value = jnp.where(
        is_live[:, :, None, None], partial_value, jnp.zeros((), partial_value.dtype)
    )
    window_count = len(offsets) * block_rows // TILE
    placed = (
        jnp.zeros((window_count, TILE, in_dim), jnp.float32)
        .at[tile_cols.reshape(-1)]
        .add(partial_value.reshape(-1, TILE, in_dim))
    )
    terms = placed.reshape(len(offsets), block_rows, in_dim)
    block_total = terms[REACH]
    for position, offset_now in enumerate(offsets):
        if offset_now != 0:
            block_total = block_total + passed_along(
                terms[position].astype(jnp.bfloat16), "blk", offset_now
            ).astype(jnp.float32)
    feature_grad = summed_on_arrival(block_total, "rep", 0)
    return (activations, feature_grad, weight_grad, bias_grad)


def solution(mesh):
    in_specs = (
        P(("blk", "rep"), None),
        P(),
        P(),
        P(("blk", "rep"), None),
        P(("blk", "rep"), None),
        P(("blk", "rep")),
        P(("blk", "rep"), None),
    )
    out_specs = (P(("blk", "rep"), None), P(("blk", "rep"), None), P(), P())
    return jax.shard_map(
        on_device, mesh=mesh, in_specs=in_specs, out_specs=out_specs, check_vma=False
    )
```

profile of v0, /device:TPU:2, one launch (start us, length us, event | category | flops | bytes accessed | tf_op | source)
XLA Modules:
  0.0 501.1 jit_solution(1405045156096830641)
XLA Ops:
  7.2 0.0 copy-start
  7.2 0.0 all-gather.2.cloned.1.call-start
  7.2 1.6 collective-permute-start
  8.8 0.8 collective-permute-start.1
  9.6 5.9 %collective-permute-done = bf16[1024,128]{1,0:T(8,128)(2,1)S(1)} collective-permute-done((bf16[1024,128]{1,0:T(8,128)(2,1)}, bf16[1024,128]{1,0:T(8,128)(2,1)S(1)}, u32[]{:S(2)}, u32[]{:S(2)}) %collective-permute-start) | collective-permute-done | bytes 262176 | tf_op jit(solution)/shard_map/ppermute | solution.py:15
  15.6 1.2 collective-permute-done.1
  16.8 1.9 pad_maximum_fusion
  18.7 0.0 all-gather.2.cloned.1.call-update
  18.7 0.7 iota_compare_fusion
  19.4 0.1 copy.15
  19.5 0.1 lt.47
  19.6 0.8 reshape.95
  20.4 0.7 compare_select_fusion
  21.1 0.1 reshape.101
  21.2 0.1 broadcast_bitcast_fusion
  21.3 37.8 %all-gather.2.cloned.1.call-done = bf16[3,4096,128]{2,1,0:T(8,128)(2,1)} async-done(((bf16[3,1024,128]{2,1,0:T(8,128)(2,1)}), bf16[3,4096,128]{2,1,0:T(8,128)(2,1)}) %all-gather.2.cloned.1.call-update) | async-done | bytes 3145744 | tf_op jit(solution)/shard_map/all_gather | solution.py:53
  59.0 10.5 %gather_fusion = bf16[256,128,128]{2,1,0:T(8,128)(2,1)} fusion(bf16[96,128,128]{2,1,0:T(8,128)(2,1)} %bitcast.41, s32[1024]{0:T(1024)S(1)} %pad_clamp_fusion), kind=kCustom, calls=%fused_computation | custom fusion | bytes 16778240 | tf_op jit(solution)/shard_map/gather | solution.py:56
  69.6 16.3 %bitcast_select_fusion = bf16[8,4096,128]{2,1,0:T(8,128)(2,1)S(1)} fusion(pred[8,4096]{1,0:T(8,128)(4,1)S(1)} %broadcast_bitcast_fusion, bf16[8,4096,128]{2,1,0:T(8,128)(2,1)} %bitcast.40), kind=kLoop, calls=%fused_computation.3 | loop fusion | flops 4194304 | bytes 16809984 | tf_op jit(solution)/shard_map/jit(_where)/select_n | solution.py:57
  85.9 0.0 copy-start.2
  85.9 0.0 copy-start.3
  85.9 5.8 %convolution_convert_fusion = bf16[8,128,128]{1,2,0:T(8,128)(2,1)S(1)} fusion(bf16[8,128,4096]{2,1,0:T(8,128)(2,1)} %bitcast.36, bf16[8,4096,128]{2,1,0:T(8,128)(2,1)S(1)} %bitcast_select_fusion), kind=kOutput, calls=%fused_computation.18 | convolution fusion | flops 1073872896 | bytes 17039360 | tf_op jit(solution)/shard_map/rik,rkf->rif/dot_general | solution.py:60
  91.7 0.0 slice-start
  91.7 0.0 slice-start.1
  91.8 2.7 convert_reduce_fusion
  94.5 0.4 convolution_convert_fusion.1
  94.9 0.6 slice-done.1
  95.6 8.1 %convolution_bitcast_fusion = f32[8,4096,128]{1,2,0:T(8,128)} fusion(bf16[8,128,128]{2,1,0:T(8,128)(2,1)S(1)} %bitcast.42, bf16[8,128,4096]{2,1,0:T(8,128)(2,1)S(1)} %bitcast.39), kind=kOutput, calls=%fused_computation.2 | convolution fusion | flops 1073741824 | bytes 25427968 | tf_op jit(solution)/shard_map/rik,rif->rkf/dot_general | solution.py:81
  103.7 17.4 %copy.17 = f32[8,4096,128]{2,1,0:T(8,128)} copy(f32[8,4096,128]{1,2,0:T(8,128)} %convolution_bitcast_fusion) | data formatting | bytes 33554432 | tf_op jit(solution)/shard_map/rik,rif->rkf/dot_general | solution.py:81
  121.0 11.6 %broadcast_select_fusion = f32[256,128,128]{2,1,0:T(8,128)} fusion(f32[256,128,128]{2,1,0:T(8,128)} %bitcast.35, pred[256]{0:T(512)(128)(4,1)S(1)} %lt.47), kind=kLoop, calls=%fused_computation.4 | loop fusion | flops 4194304 | bytes 33554688 | tf_op jit(solution)/shard_map/jit(_where)/select_n | solution.py:85
  132.7 3.4 broadcast_in_dim.45
  136.1 52.3 %scatter_fusion = f32[96,128,128]{2,1,0:T(8,128)} fusion(f32[96,128,128]{2,1,0:T(8,128)} %broadcast_in_dim.45, s32[256]{0:T(256)S(1)} %bitcast.50, f32[256,128,128]{2,1,0:T(8,128)} %broadcast_select_fusion), kind=kCustom, calls=%fused_computation.1 | custom fusion | flops 4194304 | bytes 50332672 | tf_op jit(solution)/shard_map/scatter-add | solution.py:92
  188.4 3.5 convert.4
  191.9 0.2 fusion.9
  192.1 0.5 collective-permute-start.2
  192.6 1.6 collective-permute-start.3
  194.2 1.7 slice.19
  195.9 21.5 %collective-permute-done.2 = bf16[4096,128]{1,0:T(8,128)(2,1)S(1)} collective-permute-done((bf16[4096,128]{1,0:T(8,128)(2,1)S(1)}, bf16[4096,128]{1,0:T(8,128)(2,1)S(1)}, u32[]{:S(2)}, u32[]{:S(2)}) %collective-permute-start.2) | collective-permute-done | bytes 1048608 | tf_op jit(solution)/shard_map/ppermute | solution.py:15
  217.4 3.9 collective-permute-done.3
  221.3 1.6 fusion.7
  222.9 3.6 all-to-all-start
  226.5 0.0 copy-start.1
  226.5 0.0 all-reduce.2.cloned.1.call-start
  226.6 1.0 convolution_multiply_fusion
  227.6 0.0 all-reduce.2.cloned.1.call-update
  227.6 96.5 %psum.15 = f32[512]{0:T(512)} all-reduce(f32[512]{0:T(512)S(1)} %broadcast_multiply_fusion), channel_id=1, replica_groups=mesh['blk'=64,'rep'=4] {'blk','rep'}, use_global_device_ids=true, to_apply=%region_4.5 | all-reduce | flops 512 | bytes 4096 | tf_op jit(solution)/shard_map/psum | solution.py:76
  324.1 0.9 reduce_sum.18
  325.1 167.6 %all-reduce.2.cloned.1.call-done = f32[128,512]{1,0:T(8,128)} async-done(((f32[128,512]{1,0:T(8,128)}), f32[128,512]{1,0:T(8,128)}) %all-reduce.2.cloned.1.call-update) | async-done | bytes 262160 | tf_op jit(solution)/shard_map/psum | solution.py:76
  492.6 1.7 copy.21
  (10 shorter events, 0.0 us)
Async XLA Ops:
  7.2 84.6 %copy-start = (bf16[128,512]{1,0:T(8,128)(2,1)S(1)}, bf16[128,512]{1,0:T(8,128)(2,1)}, u32[]{:S(2)}) copy-start(bf16[128,512]{1,0:T(8,128)(2,1)} %param.8) | copy-start | bytes 393220
  7.2 51.9 %all-gather.2.cloned.1.call-start = ((), (), s32[]{:S(2)}) async-start(), calls=%async_computation.1 | async-start | bytes 3932160 | tf_op jit(solution)/shard_map/all_gather | solution.py:53
  7.2 8.3 %collective-permute-start = (bf16[1024,128]{1,0:T(8,128)(2,1)}, bf16[1024,128]{1,0:T(8,128)(2,1)S(1)}, u32[]{:S(2)}, u32[]{:S(2)}) collective-permute-start(bf16[1024,128]{1,0:T(8,128)(2,1)} %param.7), channel_id=1, source_target_pairs={{0,4},{4,8},{8,12},{12,16},{16,20},{20,24},{24,28},{28,32},{32,36}... | collective-permute-start | bytes 786440 | tf_op jit(solution)/shard_map/ppermute | solution.py:15
  8.8 8.0 %collective-permute-start.1 = (bf16[1024,128]{1,0:T(8,128)(2,1)}, bf16[1024,128]{1,0:T(8,128)(2,1)S(1)}, u32[]{:S(2)}, u32[]{:S(2)}) collective-permute-start(bf16[1024,128]{1,0:T(8,128)(2,1)} %param.7), channel_id=1, source_target_pairs={{0,252},{4,0},{8,4},{12,8},{16,12},{20,16},{24,20},{28,24},{32,28}... | collective-permute-start | bytes 786440 | tf_op jit(solution)/shard_map/ppermute | solution.py:15
  85.9 5.9 %copy-start.2 = (bf16[1024,512]{1,0:T(8,128)(2,1)S(1)}, bf16[1024,512]{1,0:T(8,128)(2,1)}, u32[]{:S(2)}) copy-start(bf16[1024,512]{1,0:T(8,128)(2,1)} %param.13) | copy-start | bytes 3145732
  85.9 5.9 %copy-start.3 = (f32[512]{0:T(512)S(1)}, f32[512]{0:T(512)}, u32[]{:S(2)}) copy-start(f32[512]{0:T(512)} %param.9) | copy-start | bytes 6148
  91.7 3.2 slice-start
  91.7 3.8 slice-start.1
  192.1 25.3 %collective-permute-start.2 = (bf16[4096,128]{1,0:T(8,128)(2,1)S(1)}, bf16[4096,128]{1,0:T(8,128)(2,1)S(1)}, u32[]{:S(2)}, u32[]{:S(2)}) collective-permute-start(bf16[4096,128]{1,0:T(8,128)(2,1)S(1)} %bitcast.46), channel_id=1, source_target_pairs={{0,252},{4,0},{8,4},{12,8},{16,12},{20,16},{24,20},{28,24},{32,28}... | collective-permute-start | bytes 3145736 | tf_op jit(solution)/shard_map/ppermute | solution.py:15
  192.6 28.7 %collective-permute-start.3 = (bf16[4096,128]{1,0:T(8,128)(2,1)S(1)}, bf16[4096,128]{1,0:T(8,128)(2,1)S(1)}, u32[]{:S(2)}, u32[]{:S(2)}) collective-permute-start(bf16[4096,128]{1,0:T(8,128)(2,1)S(1)} %bitcast.45), channel_id=1, source_target_pairs={{0,4},{4,8},{8,12},{12,16},{16,20},{20,24},{24,28},{28,32},{32,36}... | collective-permute-start | bytes 3145736 | tf_op jit(solution)/shard_map/ppermute | solution.py:15
  222.9 101.3 %all-to-all-start = ((f32[4,1024,128]{2,1,0:T(8,128)}), f32[4,1024,128]{2,1,0:T(8,128)S(1)}, u32[]{:S(2)}, u32[]{:S(2)}) async-start(f32[4,1024,128]{2,1,0:T(8,128)} %bitcast.16), calls=%async_computation | async-start | bytes 4194304 | tf_op jit(solution)/shard_map/all_to_all | solution.py:25
  226.5 267.8 %copy-start.1 = (bf16[128,512]{1,0:T(8,128)(2,1)S(1)}, bf16[128,512]{1,0:T(8,128)(2,1)}, u32[]{:S(2)}) copy-start(bf16[128,512]{1,0:T(8,128)(2,1)} %param.8) | copy-start | bytes 393220
  226.5 266.1 %all-reduce.2.cloned.1.call-start = ((), (), s32[]{:S(2)}) async-start(), calls=%async_computation.2 | async-start | bytes 524288 | tf_op jit(solution)/shard_map/psum | solution.py:76
Sparse Core Ops, SparseCore 0:
  18.8 40.1 all-gather.1
  233.3 259.2 all-reduce.1
where the time goes:
time: 502 us; the launch traced here: 501 us
  waiting for transfers between devices  238 us (47%)
  blocking collectives  96.5 us (19%)
  other arithmetic  89.6 us (18%)
  local copies, waits for them, and re-layouts  36.7 us (7%)
  matrix products  18.1 us (4%)
  between operations  14.2 us (3%)
  starting transfers between devices  8.2 us (2%)
    psum x1, waiting for transfers between devices, on_device(): lax.psum((local_weight, local_bias), ('blk', 'rep'))  168 us
    psum x1, blocking collectives, on_device(): lax.psum((local_weight, local_bias), ('blk', 'rep'))  96.5 us
    scatter-add x1, other arithmetic, on_device(): placed = jnp.zeros((window_count, TILE, in_dim), jnp.float32).at[tile_col...  52.3 us
    all_gather x1, waiting for transfers between devices, on_device(): lax.all_gather(stacked, 'rep', axis=1, tiled=True).reshape(-1, in_dim)  37.8 us
    ppermute x4, waiting for transfers between devices, passed_along(): return lax.ppermute(value, axis, pairs)  32.5 us
    dot_general x1, local copies, waits for them, and re-layouts, on_device(): jnp.einsum('rik,rif->rkf', values, grad_tiles, preferred_element_type=jnp...  17.4 us
    select_n x1, other arithmetic, on_device(): jnp.where(is_live[:, :, None, None], gathered, jnp.zeros((), gathered.dty...  16.3 us
    select_n x1, other arithmetic, on_device(): jnp.where(is_live[:, :, None, None], partial_value, jnp.zeros((), partial...  11.6 us
  transfers between devices with their start and end apart: 7, of which 6 were waited for; matrix products, arithmetic and copies ran while one was open for 1% of the time, Pallas kernels for 0%

commit v1 on v0

--- a/solution.py
+++ b/solution.py
@@ -1,3 +1,4 @@
+import functools
 import math
 import jax
 import jax.numpy as jnp
@@ -7,6 +8,15 @@
 TILE = 128
 REACH = 1
 SLOTS = 32
+
+
+def link_rates_over_axis(packet, a_name, across):
+    for k0 in (across, a_name):
+        packet = jax.lax.psum(packet, axis_name=k0)
+    return packet
+
+
+sums_all_use = functools.partial(link_rates_over_axis, a_name="rep", across="blk")
 
 
 def passed_along(value, axis, steps):
@@ -73,7 +83,7 @@
         * factor
     )
     local_bias = jnp.sum(pre_grad.astype(jnp.float32), axis=0) * factor
-    weight_grad, bias_grad = lax.psum((local_weight, local_bias), ("blk", "rep"))
+    weight_grad, bias_grad = sums_all_use((local_weight, local_bias))
     row_grad = lax.dot_general(
         pre_grad, weight, (((1,), (1,)), ((), ())), preferred_element_type=jnp.float32
     ).astype(jnp.bfloat16)

time: 502 us -> 965 us (1.92)
  waiting for transfers between devices: 238 us -> 632 us
  blocking collectives: 96.5 us -> 161 us
    psum x1 -> x2, waiting for transfers between devices: 168 us -> 561 us  [link_rates_over_axis(): packet = jax.lax.psum(packet, axis_name=k0)]
    psum x1 -> x2, blocking collectives: 96.5 us -> 161 us  [link_rates_over_axis(): packet = jax.lax.psum(packet, axis_name=k0)]
  transfers between devices with their start and end apart: 7 -> 8, of which waited for: 6 -> 6; matrix products, arithmetic and copies ran while one was open for 1% -> 1% of each run, Pallas kernels for 0% -> 0%
where the time goes in v1:
time: 965 us; the launch traced here: 959 us
  waiting for transfers between devices  632 us (65%)
  blocking collectives  161 us (17%)
  other arithmetic  89.7 us (9%)
  local copies, waits for them, and re-layouts  36.7 us (4%)
  matrix products  18.1 us (2%)
  between operations  13.9 us (1%)
    psum x2, waiting for transfers between devices, link_rates_over_axis(): packet = jax.lax.psum(packet, axis_name=k0)  561 us
    psum x2, blocking collectives, link_rates_over_axis(): packet = jax.lax.psum(packet, axis_name=k0)  161 us
    scatter-add x1, other arithmetic, on_device(): placed = jnp.zeros((window_count, TILE, in_dim), jnp.float32).at[tile_col...  52.5 us
    all_gather x1, waiting for transfers between devices, on_device(): lax.all_gather(stacked, 'rep', axis=1, tiled=True).reshape(-1, in_dim)  37.8 us
    ppermute x4, waiting for transfers between devices, passed_along(): return lax.ppermute(value, axis, pairs)  32.6 us
  transfers between devices with their start and end apart: 8, of which 6 were waited for; matrix products, arithmetic and copies ran while one was open for 1% of the time, Pallas kernels for 0%

profile of v1, /device:TPU:2, one launch (start us, length us, event | category | flops | bytes accessed | tf_op | source)
XLA Modules:
  0.0 959.4 jit_solution(11307551306831335850)
XLA Ops:
  7.2 0.0 copy-start
  7.2 0.0 all-gather.2.cloned.1.call-start
  7.2 1.6 collective-permute-start
  8.8 0.8 collective-permute-start.1
  9.6 5.9 collective-permute-done
  15.6 1.2 collective-permute-done.1
  16.8 1.9 pad_maximum_fusion
  18.7 0.0 all-gather.2.cloned.1.call-update
  18.7 0.7 iota_compare_fusion
  19.4 0.1 copy.15
  19.5 0.1 lt.47
  19.6 0.8 reshape.95
  20.4 0.7 compare_select_fusion
  21.1 0.1 reshape.101
  21.2 0.1 broadcast_bitcast_fusion
  21.3 37.8 %all-gather.2.cloned.1.call-done = bf16[3,4096,128]{2,1,0:T(8,128)(2,1)} async-done(((bf16[3,1024,128]{2,1,0:T(8,128)(2,1)}), bf16[3,4096,128]{2,1,0:T(8,128)(2,1)}) %all-gather.2.cloned.1.call-update) | async-done | bytes 3145744 | tf_op jit(solution)/shard_map/all_gather | solution.py:63
  59.0 10.5 %gather_fusion = bf16[256,128,128]{2,1,0:T(8,128)(2,1)} fusion(bf16[96,128,128]{2,1,0:T(8,128)(2,1)} %bitcast.41, s32[1024]{0:T(1024)S(1)} %pad_clamp_fusion), kind=kCustom, calls=%fused_computation | custom fusion | bytes 16778240 | tf_op jit(solution)/shard_map/gather | solution.py:66
  69.5 16.3 %bitcast_select_fusion = bf16[8,4096,128]{2,1,0:T(8,128)(2,1)S(1)} fusion(pred[8,4096]{1,0:T(8,128)(4,1)S(1)} %broadcast_bitcast_fusion, bf16[8,4096,128]{2,1,0:T(8,128)(2,1)} %bitcast.40), kind=kLoop, calls=%fused_computation.3 | loop fusion | flops 4194304 | bytes 16809984 | tf_op jit(solution)/shard_map/jit(_where)/select_n | solution.py:67
  85.9 5.8 convolution_convert_fusion
  91.7 0.0 slice-start
  91.7 2.7 convert_reduce_fusion
  94.5 0.4 convolution_convert_fusion.1
  94.9 0.6 slice-done.1
  95.5 8.1 convolution_bitcast_fusion
  103.6 17.4 %copy.17 = f32[8,4096,128]{2,1,0:T(8,128)} copy(f32[8,4096,128]{1,2,0:T(8,128)} %convolution_bitcast_fusion) | data formatting | bytes 33554432 | tf_op jit(solution)/shard_map/rik,rif->rkf/dot_general | solution.py:91
  121.0 11.6 %broadcast_select_fusion = f32[256,128,128]{2,1,0:T(8,128)} fusion(f32[256,128,128]{2,1,0:T(8,128)} %bitcast.35, pred[256]{0:T(512)(128)(4,1)S(1)} %lt.47), kind=kLoop, calls=%fused_computation.4 | loop fusion | flops 4194304 | bytes 33554688 | tf_op jit(solution)/shard_map/jit(_where)/select_n | solution.py:95
  132.6 3.4 broadcast_in_dim.45
  136.1 52.5 %scatter_fusion = f32[96,128,128]{2,1,0:T(8,128)} fusion(f32[96,128,128]{2,1,0:T(8,128)} %broadcast_in_dim.45, s32[256]{0:T(256)S(1)} %bitcast.50, f32[256,128,128]{2,1,0:T(8,128)} %broadcast_select_fusion), kind=kCustom, calls=%fused_computation.1 | custom fusion | flops 4194304 | bytes 50332672 | tf_op jit(solution)/shard_map/scatter-add | solution.py:102
  188.5 3.5 convert.4
  192.0 0.2 fusion.9
  192.2 0.5 collective-permute-start.2
  192.7 1.6 collective-permute-start.3
  194.3 1.7 slice.19
  196.0 21.4 %collective-permute-done.2 = bf16[4096,128]{1,0:T(8,128)(2,1)S(1)} collective-permute-done((bf16[4096,128]{1,0:T(8,128)(2,1)S(1)}, bf16[4096,128]{1,0:T(8,128)(2,1)S(1)}, u32[]{:S(2)}, u32[]{:S(2)}) %collective-permute-start.2) | collective-permute-done | bytes 1048608 | tf_op jit(solution)/shard_map/ppermute | solution.py:25
  217.5 4.0 collective-permute-done.3
  221.5 1.6 fusion.7
  223.1 3.6 all-to-all-start
  226.7 0.0 copy-start.1
  226.7 0.0 all-reduce.3.cloned.1.call-start
  226.8 1.0 convolution_multiply_fusion
  227.8 0.0 all-reduce.3.cloned.1.call-update
  227.8 0.0 all-reduce.5.cloned.1.call-start
  227.9 561.4 %all-reduce.3.cloned.1.call-done = f32[128,512]{1,0:T(8,128)} async-done(((f32[128,512]{1,0:T(8,128)}), f32[128,512]{1,0:T(8,128)}) %all-reduce.3.cloned.1.call-update) | async-done | bytes 262160 | tf_op jit(solution)/shard_map/psum | solution.py:15
  789.3 0.0 all-reduce.5.cloned.1.call-update
  789.3 153.3 %psum.30 = f32[512]{0:T(512)S(1)} all-reduce(f32[512]{0:T(512)S(1)} %broadcast_multiply_fusion), channel_id=1, replica_groups=mesh['blk'=64,'rep'=4] {'blk'}, use_global_device_ids=true, to_apply=%region_5.6 | all-reduce | flops 512 | bytes 4096 | tf_op jit(solution)/shard_map/psum | solution.py:15
  942.6 7.7 psum.31
  950.3 0.9 reduce_sum.18
  951.2 1.7 copy.22
  (14 shorter events, 0.0 us)
Async XLA Ops:
  7.2 84.5 %copy-start = (bf16[128,512]{1,0:T(8,128)(2,1)S(1)}, bf16[128,512]{1,0:T(8,128)(2,1)}, u32[]{:S(2)}) copy-start(bf16[128,512]{1,0:T(8,128)(2,1)} %param.8) | copy-start | bytes 393220
  7.2 51.9 %all-gather.2.cloned.1.call-start = ((), (), s32[]{:S(2)}) async-start(), calls=%async_computation.1 | async-start | bytes 3932160 | tf_op jit(solution)/shard_map/all_gather | solution.py:63
  7.2 8.3 collective-permute-start
  8.8 8.0 collective-permute-start.1
  85.8 5.9 copy-start.2
  85.9 5.9 copy-start.3
  91.7 3.2 slice-start
  91.7 3.8 slice-start.1
  192.2 25.3 %collective-permute-start.2 = (bf16[4096,128]{1,0:T(8,128)(2,1)S(1)}, bf16[4096,128]{1,0:T(8,128)(2,1)S(1)}, u32[]{:S(2)}, u32[]{:S(2)}) collective-permute-start(bf16[4096,128]{1,0:T(8,128)(2,1)S(1)} %bitcast.46), channel_id=1, source_target_pairs={{0,252},{4,0},{8,4},{12,8},{16,12},{20,16},{24,20},{28,24},{32,28}... | collective-permute-start | bytes 3145736 | tf_op jit(solution)/shard_map/ppermute | solution.py:25
  192.7 28.7 %collective-permute-start.3 = (bf16[4096,128]{1,0:T(8,128)(2,1)S(1)}, bf16[4096,128]{1,0:T(8,128)(2,1)S(1)}, u32[]{:S(2)}, u32[]{:S(2)}) collective-permute-start(bf16[4096,128]{1,0:T(8,128)(2,1)S(1)} %bitcast.45), channel_id=1, source_target_pairs={{0,4},{4,8},{8,12},{12,16},{16,20},{20,24},{24,28},{28,32},{32,36}... | collective-permute-start | bytes 3145736 | tf_op jit(solution)/shard_map/ppermute | solution.py:25
  223.1 727.2 %all-to-all-start = ((f32[4,1024,128]{2,1,0:T(8,128)}), f32[4,1024,128]{2,1,0:T(8,128)S(1)}, u32[]{:S(2)}, u32[]{:S(2)}) async-start(f32[4,1024,128]{2,1,0:T(8,128)} %bitcast.16), calls=%async_computation | async-start | bytes 4194304 | tf_op jit(solution)/shard_map/all_to_all | solution.py:35
  226.7 726.2 %copy-start.1 = (bf16[128,512]{1,0:T(8,128)(2,1)S(1)}, bf16[128,512]{1,0:T(8,128)(2,1)}, u32[]{:S(2)}) copy-start(bf16[128,512]{1,0:T(8,128)(2,1)} %param.8) | copy-start | bytes 393220
  226.7 562.6 %all-reduce.3.cloned.1.call-start = ((), (), s32[]{:S(2)}) async-start(), calls=%async_computation.2 | async-start | bytes 524288 | tf_op jit(solution)/shard_map/psum | solution.py:15
  227.8 723.4 %all-reduce.5.cloned.1.call-start = ((), (), s32[]{:S(2)}) async-start(), calls=%async_computation.3 | async-start | bytes 524288 | tf_op jit(solution)/shard_map/psum | solution.py:15
Sparse Core Ops, SparseCore 0:
  18.8 40.1 all-gather.1
  230.7 558.5 all-reduce.2
  791.9 44.4 all-reduce.4
